TPU v7x, 512 devices: a whole 4x8x8 slice. The times are simulated.
512 devices in a mesh: pipe: 8 (over y_lo, core), tensor: 64 (over y_hi, x, z).
Axes of the slice: x: 4, y: 8 (y_hi: 2, y_lo: 4; y = y_hi * 4 + y_lo), z: 8, core: 2. Of those that a mesh axis runs over, the one named last changes fastest.
Arguments:
- output_gradient: bfloat16 [8, 64, 2, 64, 1024], P('pipe', 'tensor'), may hold values from -6 to 6
- forward_input: bfloat16 [8, 2, 512, 8192], P('pipe', None, None, 'tensor'), may hold values from -6 to 6
- saved_rank_outputs: bfloat16 [8, 2, 512, 64], P('pipe', None, 'tensor'), may hold values from -6 to 6
- projection_weight: bfloat16 [8, 64, 1024, 1024], P('pipe', 'tensor'), may hold values from -0.0625 to 0.0625
- adapter_down_maps: bfloat16 [8, 8, 64, 8192], P('pipe', None, None, 'tensor'), may hold values from -0.75 to 0.75
- adapter_up_maps: bfloat16 [8, 64, 8, 8, 1024], P('pipe', 'tensor'), may hold values from -0.0625 to 0.0625
- segment_adapter_class: int32 [8, 2, 4], P('pipe'), may hold values from 0 to 7
- live_segment_table: int32 [8, 2], P('pipe'), may hold values from 1 to 4, as said below
Outputs:
- grad_prev: bfloat16 [8, 2, 512, 8192], P('pipe', None, None, 'tensor')
- down_map_gradient: bfloat16 [8, 8, 64, 8192], P('pipe', None, None, 'tensor')
- up_map_gradient: bfloat16 [8, 64, 8, 8, 1024], P('pipe', 'tensor')
Inputs may be any that keep to these rules, and one draw needn't show every extreme that they name: The first live_segment_table segments of a microbatch are live; some microbatch has all 4 live.
All inputs are finite; a program needn't handle non-finite values.
Results may differ from a plain program's by a relative error of at most 0.0049.
Values may be sent and summed in bfloat16 or wider, within the bound.
A program may use at most 64 MiB of HBM per device.

v0:
```python
import jax
import jax.numpy as jnp
from jax import lax
from jax.sharding import PartitionSpec as P

SEG = 128


def partner(value, axis, apart):
    mask = 2**apart
    pairs = [(source, source ^ mask) for source in range(lax.axis_size(axis))]
    return lax.ppermute(value, axis, pairs)


def shifted(block, axis, distance):
    devices = range(lax.axis_size(axis))
    route = [((i - distance) % len(devices), i) for i in devices]
    return lax.ppermute(block, axis, route)


def choose_segment_rows(class_indicator, segment_lookup):
    return jnp.einsum(
        "pzw,wlq->pzlq", class_indicator, segment_lookup, preferred_element_type=jnp.float32
    ).astype(jnp.bfloat16)


def shards(
    output_gradient,
    forward_input,
    saved_rank_outputs,
    projection_weight,
    adapter_down_maps,
    adapter_up_maps,
    segment_adapter_class,
    live_segment_table,
):
    grad_tile = output_gradient[0, 0]
    micro_count, tile_rows, tile_cols = grad_tile.shape
    weight = projection_weight[0, 0]
    up_matrix_tile = adapter_up_maps[0, 0]
    rank_part = up_matrix_tile.shape[1]
    rank_extent = adapter_down_maps.shape[2]
    local_portion = adapter_down_maps.shape[3]
    group_size = lax.axis_size("tensor")
    total_bits = group_size.bit_length() - 1
    low_size = min(group_size, 8)
    low_bits = low_size.bit_length() - 1
    high_size = group_size // low_size
    position = lax.axis_index("tensor")
    high_index = position // low_size
    batch_rows = tile_rows * high_size
    seg_count = batch_rows // SEG
    row_ids = high_index * tile_rows + jnp.arange(tile_rows, dtype=jnp.int32)
    live_count = live_segment_table[0]
    keep_rows = (row_ids // SEG)[None, :] < live_count[:, None]
    masked_tile = jnp.where(keep_rows[:, :, None], grad_tile, jnp.zeros_like(grad_tile))
    gathered = masked_tile
    for level in range(low_bits, total_bits):
        received = partner(gathered, "tensor", level)
        leading = position >> level & 1 == 0
        gathered = jnp.where(
            leading,
            jnp.concatenate([gathered, received], 1),
            jnp.concatenate([received, gathered], 1),
        )
    products = jnp.einsum("mrd,id->mri", gathered, weight, preferred_element_type=jnp.float32)
    reduced = products
    for level in reversed(range(low_bits)):
        half_cols = reduced.shape[2] // 2
        lower_half = reduced[:, :, :half_cols]
        upper_half = reduced[:, :, half_cols:]
        upper_side = position >> level & 1 == 1
        kept_half = jnp.where(upper_side, upper_half, lower_half)
        sent_half = jnp.where(upper_side, lower_half, upper_half)
        reduced = kept_half + partner(sent_half, "tensor", level)
    classes = segment_adapter_class[0]
    class_indicator = (
        classes[:, :, None] == jnp.arange(up_matrix_tile.shape[0], dtype=jnp.int32)[None, None, :]
    ).astype(jnp.bfloat16)
    selected_up_matrix = choose_segment_rows(class_indicator, up_matrix_tile)
    grad_segs = gathered.reshape(micro_count, seg_count, SEG, tile_cols)
    partial_rank = jnp.einsum(
        "mskd,msrd->mskr", grad_segs, selected_up_matrix, preferred_element_type=jnp.float32
    )
    padded_rank = jnp.zeros((micro_count, seg_count, SEG, rank_extent), jnp.float32)
    padded_rank = lax.dynamic_update_slice_in_dim(
        padded_rank, partial_rank, high_index * rank_part, 3
    )
    lowrank = lax.psum(padded_rank, "tensor").astype(jnp.bfloat16)
    selected_down_matrix = choose_segment_rows(class_indicator, adapter_down_maps[0])
    adapter = jnp.einsum(
        "mskr,msrd->mskd", lowrank, selected_down_matrix, preferred_element_type=jnp.float32
    )
    input_gradient = (reduced + adapter.reshape(micro_count, batch_rows, local_portion)).astype(
        jnp.bfloat16
    )
    grad_prev = shifted(input_gradient, "pipe", -1)
    inputs_seg = forward_input[0].reshape(micro_count, seg_count, SEG, local_portion)
    segment_down_matrix = jnp.einsum(
        "mskr,mskd->msrd", lowrank, inputs_seg, preferred_element_type=jnp.float32
    )
    hidden = lax.all_gather(saved_rank_outputs[0], "tensor", axis=1, tiled=True)
    hidden_part = lax.dynamic_slice_in_dim(hidden, high_index * rank_part, rank_part, 2)
    hidden_seg = hidden_part.reshape(micro_count, seg_count, SEG, rank_part)
    segment_up_matrix = jnp.einsum(
        "mskr,mskd->msrd", hidden_seg, grad_segs, preferred_element_type=jnp.float32
    )
    wide_class_indicator = class_indicator.astype(jnp.float32)
    down_map_gradient = jnp.einsum(
        "exk,exlq->klq", wide_class_indicator, segment_down_matrix, precision=lax.Precision.HIGHEST
    ).astype(jnp.bfloat16)
    up_map_gradient = jnp.einsum(
        "exk,exlq->klq", wide_class_indicator, segment_up_matrix, precision=lax.Precision.HIGHEST
    ).astype(jnp.bfloat16)
    return (grad_prev[None], down_map_gradient[None], up_map_gradient[None, None])


def solution(mesh):
    in_specs = (
        P("pipe", "tensor", None, None, None),
        P("pipe", None, None, "tensor"),
        P("pipe", None, "tensor", None),
        P("pipe", "tensor", None, None),
        P("pipe", None, None, "tensor"),
        P("pipe", "tensor", None, None, None),
        P("pipe", None, None),
        P("pipe", None),
    )
    out_specs = (
        P("pipe", None, None, "tensor"),
        P("pipe", None, None, "tensor"),
        P("pipe", "tensor", None, None, None),
    )
    return jax.shard_map(shards, mesh=mesh, in_specs=in_specs, out_specs=out_specs, check_vma=False)
```

profile of v0, /device:TPU:9, one launch (start us, length us, event | category | flops | bytes accessed | tf_op | source)
XLA Modules:
  0.0 877.9 jit_solution(1295151885727014478)
XLA Ops:
  0.6 0.0 copy-start
  0.7 0.9 broadcast_compare_fusion
  1.5 1.0 bitcast_select_fusion
  2.6 3.1 collective-permute-start
  5.7 6.0 collective-permute-done
  11.7 0.1 maximum_select_fusion.2
  11.8 0.0 copy-start.6
  11.8 4.7 collective-permute-start.1
  16.5 0.0 copy-done.6
  16.5 10.8 %collective-permute-done.1 = bf16[2,128,1024]{2,1,0:T(8,128)(2,1)} collective-permute-done((bf16[2,128,1024]{2,1,0:T(8,128)(2,1)S(1)}, bf16[2,128,1024]{2,1,0:T(8,128)(2,1)}, u32[]{:S(2)}, u32[]{:S(2)}) %collective-permute-start.1) | collective-permute-done | bytes 524320 | tf_op jit(solution)/shard_map/ppermute | solution.py:12
  27.3 2.1 maximum_select_fusion.1
  29.4 6.6 collective-permute-start.2
  35.9 43.0 %collective-permute-done.2 = bf16[2,256,1024]{2,1,0:T(8,128)(2,1)} collective-permute-done((bf16[2,256,1024]{2,1,0:T(8,128)(2,1)S(1)}, bf16[2,256,1024]{2,1,0:T(8,128)(2,1)}, u32[]{:S(2)}, u32[]{:S(2)}) %collective-permute-start.2) | collective-permute-done | bytes 1048608 | tf_op jit(solution)/shard_map/ppermute | solution.py:12
  78.9 2.6 maximum_select_fusion
  81.5 0.0 copy-done
  81.5 0.0 copy-start.1
  81.5 2.4 fusion
  83.9 0.0 copy-done.1
  83.9 0.0 copy-start.5
  83.9 0.0 copy-start.12
  83.9 2.2 slice_select_fusion
  86.1 0.5 copy-done.5
  86.7 10.6 %collective-permute-start.3 = (f32[2,512,512]{2,1,0:T(8,128)}, f32[2,512,512]{2,1,0:T(8,128)}, u32[]{:S(2)}, u32[]{:S(2)}) collective-permute-start(f32[2,512,512]{2,1,0:T(8,128)} %slice_select_fusion), channel_id=1, source_target_pairs={{0,4},{1,5},{2,6},{3,7},{4,0},{5,1},{6,2},{7,3},{8,12},{9,13},{10,... | collective-permute-start | bytes 6291464 | tf_op jit(solution)/shard_map/ppermute | solution.py:12
  97.3 0.0 copy-done.12
  97.3 272.6 %all-gather = bf16[1,2,512,64]{3,2,1,0:T(8,128)(2,1)S(1)} all-gather(bf16[1,2,8,64]{3,2,1,0:T(8,128)(2,1)S(1)} %copy-done.12), channel_id=2, replica_groups=mesh['pipe'=8,'tensor'=64] {'tensor'}, dimensions={2}, use_global_device_ids=true | all-gather | bytes 133120 | tf_op jit(solution)/shard_map/all_gather | solution.py:102
  370.0 0.0 collective-permute-done.3
  370.0 3.6 select_add_fusion
  373.6 0.0 copy-start.3
  373.6 1.3 copy-done.3
  374.9 0.0 copy-start.10
  374.9 0.0 copy-start.11
  374.9 0.1 slice_select_fusion.1
  375.1 1.9 collective-permute-start.4
  377.0 0.1 constant_dynamic-slice_fusion
  377.1 0.0 copy-start.2
  377.1 0.0 copy-done.10
  377.2 0.0 copy-done.11
  377.2 0.9 fusion.10
  378.1 1.1 fusion.12
  379.2 0.0 copy-start.4
  379.3 2.4 convolution_dynamic-update-slice_fusion
  381.6 0.7 copy-done.7
  382.4 0.0 copy-done.2
  382.4 0.4 fusion.27
  382.8 14.4 %collective-permute-done.4 = f32[2,512,256]{2,1,0:T(8,128)} collective-permute-done((f32[2,512,256]{2,1,0:T(8,128)S(1)}, f32[2,512,256]{2,1,0:T(8,128)}, u32[]{:S(2)}, u32[]{:S(2)}) %collective-permute-start.4) | collective-permute-done | bytes 1048608 | tf_op jit(solution)/shard_map/ppermute | solution.py:12
  397.2 0.0 copy-done.4
  397.2 1.4 select_add_fusion.1
  398.6 0.0 copy-start.8
  398.6 0.8 slice_select_fusion.2
  399.4 1.9 collective-permute-start.5
  401.4 0.6 fusion.4
  401.9 0.7 copy.12
  402.7 0.0 copy-done.8
  402.7 374.2 %all-reduce.1 = bf16[2,4,128,64]{2,3,1,0:T(8,128)(2,1)S(1)} all-reduce(f32[2,4,128,64]{2,3,1,0:T(8,128)S(1)} %copy-done.8), channel_id=1, replica_groups=mesh['pipe'=8,'tensor'=64] {'tensor'}, use_global_device_ids=true, to_apply=%region_0.1 | all-reduce | flops 65536 | bytes 393216 | tf_op jit(solution)/shard_map/psum | solution.py:89
  776.9 1.2 fusion.9
  778.1 0.0 collective-permute-done.5
  778.1 1.2 fusion.6
  779.3 90.0 %collective-permute-start.6 = (bf16[2,512,128]{2,1,0:T(8,128)(2,1)S(1)}, bf16[2,512,128]{2,1,0:T(8,128)(2,1)S(1)}, u32[]{:S(2)}, u32[]{:S(2)}) collective-permute-start(bf16[2,512,128]{2,1,0:T(8,128)(2,1)S(1)} %fusion.6), channel_id=1, source_target_pairs={{64,0},{128,64},{192,128},{256,192},{320,256},{384,320},{448,384},... | collective-permute-start | bytes 786440 | tf_op jit(solution)/shard_map/ppermute | solution.py:18
  869.3 0.0 copy-done.9
  869.3 0.2 fusion.28
  869.5 0.6 fusion.5
  870.1 0.7 copy.11
  870.8 6.4 collective-permute-done.6
  877.2 0.7 copy.38
  (4 shorter events, 0.0 us)
Async XLA Ops:
  0.6 80.9 %copy-start = (bf16[1,1,1024,1024]{3,2,1,0:T(8,128)(2,1)S(1)}, bf16[1,1,1024,1024]{3,2,1,0:T(8,128)(2,1)}, u32[]{:S(2)}) copy-start(bf16[1,1,1024,1024]{3,2,1,0:T(8,128)(2,1)} %param.11) | copy-start | bytes 6291460
  2.6 9.1 %collective-permute-start = (bf16[2,64,1024]{2,1,0:T(8,128)(2,1)S(1)}, bf16[2,64,1024]{2,1,0:T(8,128)(2,1)S(1)}, u32[]{:S(2)}, u32[]{:S(2)}) collective-permute-start(bf16[2,64,1024]{2,1,0:T(8,128)(2,1)S(1)} %bitcast_select_fusion), channel_id=1, source_target_pairs={{0,8},{1,9},{2,10},{3,11},{4,12},{5,13},{6,14},{7,15},{8,0},{9,1},... | collective-permute-start | bytes 786440 | tf_op jit(solution)/shard_map/ppermute | solution.py:12
  11.8 4.7 copy-start.6
  11.8 15.5 %collective-permute-start.1 = (bf16[2,128,1024]{2,1,0:T(8,128)(2,1)S(1)}, bf16[2,128,1024]{2,1,0:T(8,128)(2,1)}, u32[]{:S(2)}, u32[]{:S(2)}) collective-permute-start(bf16[2,128,1024]{2,1,0:T(8,128)(2,1)S(1)} %maximum_select_fusion.2), channel_id=1, source_target_pairs={{0,16},{1,17},{2,18},{3,19},{4,20},{5,21},{6,22},{7,23},{8,24},{9,... | collective-permute-start | bytes 1572872 | tf_op jit(solution)/shard_map/ppermute | solution.py:12
  29.4 49.6 %collective-permute-start.2 = (bf16[2,256,1024]{2,1,0:T(8,128)(2,1)S(1)}, bf16[2,256,1024]{2,1,0:T(8,128)(2,1)}, u32[]{:S(2)}, u32[]{:S(2)}) collective-permute-start(bf16[2,256,1024]{2,1,0:T(8,128)(2,1)S(1)} %maximum_select_fusion.1), channel_id=1, source_target_pairs={{0,32},{1,33},{2,34},{3,35},{4,36},{5,37},{6,38},{7,39},{8,40},{9,... | collective-permute-start | bytes 3145736 | tf_op jit(solution)/shard_map/ppermute | solution.py:12
  81.5 2.4 copy-start.1
  83.9 2.7 copy-start.5
  83.9 13.4 %copy-start.12 = (bf16[1,2,8,64]{3,2,1,0:T(8,128)(2,1)S(1)}, bf16[1,2,8,64]{3,2,1,0:T(8,128)(2,1)}, u32[]{:S(2)}) copy-start(bf16[1,2,8,64]{3,2,1,0:T(8,128)(2,1)} %param.10) | copy-start | bytes 6148
  86.7 283.3 %collective-permute-start.3 = (f32[2,512,512]{2,1,0:T(8,128)}, f32[2,512,512]{2,1,0:T(8,128)}, u32[]{:S(2)}, u32[]{:S(2)}) collective-permute-start(f32[2,512,512]{2,1,0:T(8,128)} %slice_select_fusion), channel_id=1, source_target_pairs={{0,4},{1,5},{2,6},{3,7},{4,0},{5,1},{6,2},{7,3},{8,12},{9,13},{10,... | collective-permute-start | bytes 6291464 | tf_op jit(solution)/shard_map/ppermute | solution.py:12
  373.6 1.3 copy-start.3
  374.9 2.2 copy-start.10
  374.9 2.2 copy-start.11
  375.1 22.1 %collective-permute-start.4 = (f32[2,512,256]{2,1,0:T(8,128)S(1)}, f32[2,512,256]{2,1,0:T(8,128)}, u32[]{:S(2)}, u32[]{:S(2)}) collective-permute-start(f32[2,512,256]{2,1,0:T(8,128)S(1)} %slice_select_fusion.1), channel_id=1, source_target_pairs={{0,2},{1,3},{2,0},{3,1},{4,6},{5,7},{6,4},{7,5},{8,10},{9,11},{10,... | collective-permute-start | bytes 3145736 | tf_op jit(solution)/shard_map/ppermute | solution.py:12
  377.1 5.2 copy-start.2
  379.2 17.9 %copy-start.4 = (f32[2,512,512]{2,1,0:T(8,128)S(1)}, f32[2,512,512]{2,1,0:T(8,128)}, u32[]{:S(2)}) copy-start(f32[2,512,512]{2,1,0:T(8,128)} %copy-done.3) | copy-start | bytes 6291460
  381.6 0.7 copy-start.7
  398.6 4.1 copy-start.8
  399.4 378.6 %collective-permute-start.5 = (f32[2,512,128]{2,1,0:T(8,128)}, f32[2,512,128]{2,1,0:T(8,128)}, u32[]{:S(2)}, u32[]{:S(2)}) collective-permute-start(f32[2,512,128]{2,1,0:T(8,128)} %slice_select_fusion.2), channel_id=1, source_target_pairs={{0,1},{1,0},{2,3},{3,2},{4,5},{5,4},{6,7},{7,6},{8,9},{9,8},{10,11... | collective-permute-start | bytes 1572872 | tf_op jit(solution)/shard_map/ppermute | solution.py:12
  776.9 92.5 %copy-start.9 = (bf16[1,2,512,128]{3,2,1,0:T(8,128)(2,1)S(1)}, bf16[1,2,512,128]{3,2,1,0:T(8,128)(2,1)}, u32[]{:S(2)}) copy-start(bf16[1,2,512,128]{3,2,1,0:T(8,128)(2,1)} %param.9) | copy-start | bytes 786436
  779.3 97.9 %collective-permute-start.6 = (bf16[2,512,128]{2,1,0:T(8,128)(2,1)S(1)}, bf16[2,512,128]{2,1,0:T(8,128)(2,1)S(1)}, u32[]{:S(2)}, u32[]{:S(2)}) collective-permute-start(bf16[2,512,128]{2,1,0:T(8,128)(2,1)S(1)} %fusion.6), channel_id=1, source_target_pairs={{64,0},{128,64},{192,128},{256,192},{320,256},{384,320},{448,384},... | collective-permute-start | bytes 786440 | tf_op jit(solution)/shard_map/ppermute | solution.py:18
where the time goes:
time: 878 us
  blocking collectives  647 us (74%)
  starting transfers between devices  119 us (14%)
  waiting for transfers between devices  80.5 us (9%)
  other arithmetic  16.1 us (2%)
  matrix products  9.77 us (1%)
    psum x1, blocking collectives, shards(): lowrank = lax.psum(padded_rank, 'tensor').astype(jnp.bfloat16)  374 us
    all_gather x1, blocking collectives, shards(): hidden = lax.all_gather(saved_rank_outputs[0], 'tensor', axis=1, tiled=True)  273 us
    ppermute x1, starting transfers between devices, shifted(): return lax.ppermute(block, axis, route)  90 us
    ppermute x6, waiting for transfers between devices, partner(): return lax.ppermute(value, axis, pairs)  74.1 us
    ppermute x6, starting transfers between devices, partner(): return lax.ppermute(value, axis, pairs)  28.8 us
  transfers between devices with their start and end apart: 7, of which 5 were waited for; matrix products, arithmetic and copies ran while one was open for 1% of the time, Pallas kernels for 0%

commit v1 on v0

--- a/solution.py
+++ b/solution.py
@@ -99,7 +99,9 @@
     segment_down_matrix = jnp.einsum(
         "mskr,mskd->msrd", lowrank, inputs_seg, preferred_element_type=jnp.float32
     )
-    hidden = lax.all_gather(saved_rank_outputs[0], "tensor", axis=1, tiled=True)
+    part = saved_rank_outputs[0]
+    sent = jnp.stack([part] * lax.axis_size("tensor"))
+    hidden = jnp.concatenate(lax.all_to_all(sent, "tensor", 0, 0), axis=1)
     hidden_part = lax.dynamic_slice_in_dim(hidden, high_index * rank_part, rank_part, 2)
     hidden_seg = hidden_part.reshape(micro_count, seg_count, SEG, rank_part)
     segment_up_matrix = jnp.einsum(

time: 878 us -> 701 us (0.80)
  the two profiles are of different devices: /device:TPU:9 before, /device:TPU:17 now
where the time goes in v1:
time: 701 us; the launch traced here: 700 us
  blocking collectives  377 us (54%)
  waiting for transfers between devices  150 us (21%)
  starting transfers between devices  140 us (20%)
  other arithmetic  16.1 us (2%)
  matrix products  9.54 us (1%)
    psum x1, blocking collectives, shards(): lowrank = lax.psum(padded_rank, 'tensor').astype(jnp.bfloat16)  377 us
    ppermute x6, waiting for transfers between devices, partner(): return lax.ppermute(value, axis, pairs)  146 us
    ppermute x6, starting transfers between devices, partner(): return lax.ppermute(value, axis, pairs)  72.5 us
    ppermute x1, starting transfers between devices, shifted(): return lax.ppermute(block, axis, route)  58.6 us
  transfers between devices with their start and end apart: 8, of which 6 were waited for; matrix products, arithmetic and copies ran while one was open for 2% of the time, Pallas kernels for 0%

profile of v1, /device:TPU:17, one launch (start us, length us, event | category | flops | bytes accessed | tf_op | source)
XLA Modules:
  0.0 700.0 jit_solution(15706163343478199111)
XLA Ops:
  0.6 0.0 copy-start
  0.7 0.9 broadcast_compare_fusion
  1.5 1.0 bitcast_select_fusion
  2.6 3.1 collective-permute-start
  5.7 6.0 collective-permute-done
  11.7 0.1 maximum_select_fusion.2
  11.8 0.0 copy-start.6
  11.8 4.7 collective-permute-start.1
  16.5 0.0 copy-done.6
  16.5 10.8 %collective-permute-done.1 = bf16[2,128,1024]{2,1,0:T(8,128)(2,1)} collective-permute-done((bf16[2,128,1024]{2,1,0:T(8,128)(2,1)S(1)}, bf16[2,128,1024]{2,1,0:T(8,128)(2,1)}, u32[]{:S(2)}, u32[]{:S(2)}) %collective-permute-start.1) | collective-permute-done | bytes 524320 | tf_op jit(solution)/shard_map/ppermute | solution.py:12
  27.3 2.1 maximum_select_fusion.1
  29.4 5.7 collective-permute-start.2
  35.0 47.8 %collective-permute-done.2 = bf16[2,256,1024]{2,1,0:T(8,128)(2,1)} collective-permute-done((bf16[2,256,1024]{2,1,0:T(8,128)(2,1)S(1)}, bf16[2,256,1024]{2,1,0:T(8,128)(2,1)}, u32[]{:S(2)}, u32[]{:S(2)}) %collective-permute-start.2) | collective-permute-done | bytes 1048608 | tf_op jit(solution)/shard_map/ppermute | solution.py:12
  82.8 2.6 maximum_select_fusion
  85.4 0.0 copy-done
  85.4 0.0 copy-start.1
  85.4 2.4 fusion
  87.8 0.0 copy-done.1
  87.8 0.0 copy-start.5
  87.8 0.0 copy-start.11
  87.8 0.0 copy-start.8
  87.8 0.0 copy-start.10
  87.9 2.2 slice_select_fusion
  90.1 0.5 copy-done.5
  90.6 10.6 %collective-permute-start.3 = (f32[2,512,512]{2,1,0:T(8,128)}, f32[2,512,512]{2,1,0:T(8,128)}, u32[]{:S(2)}, u32[]{:S(2)}) collective-permute-start(f32[2,512,512]{2,1,0:T(8,128)} %slice_select_fusion), channel_id=1, source_target_pairs={{0,4},{1,5},{2,6},{3,7},{4,0},{5,1},{6,2},{7,3},{8,12},{9,13},{10,... | collective-permute-start | bytes 6291464 | tf_op jit(solution)/shard_map/ppermute | solution.py:12
  101.2 0.0 copy-done.11
  101.2 0.8 reshape.85
  102.1 9.3 %all-to-all-start = ((bf16[64,2,512]{2,1,0:T(2,128)(2,1)}), bf16[64,2,512]{2,1,0:T(2,128)(2,1)S(1)}, u32[]{:S(2)}, u32[]{:S(2)}) async-start(bf16[64,2,512]{2,1,0:T(2,128)(2,1)} %reshape.85), calls=%async_computation | async-start | bytes 262144 | tf_op jit(solution)/shard_map/all_to_all | solution.py:104
  111.5 0.0 copy-done.8
  111.5 0.0 copy-done.10
  111.5 0.9 convolution_convert_fusion
  112.4 40.1 %collective-permute-done.3 = f32[2,512,512]{2,1,0:T(8,128)} collective-permute-done((f32[2,512,512]{2,1,0:T(8,128)}, f32[2,512,512]{2,1,0:T(8,128)}, u32[]{:S(2)}, u32[]{:S(2)}) %collective-permute-start.3) | collective-permute-done | bytes 2097184 | tf_op jit(solution)/shard_map/ppermute | solution.py:12
  152.4 3.6 select_add_fusion
  156.0 0.0 copy-start.3
  156.0 1.3 copy-done.3
  157.4 0.1 slice_select_fusion.1
  157.5 46.5 %collective-permute-start.4 = (f32[2,512,256]{2,1,0:T(8,128)S(1)}, f32[2,512,256]{2,1,0:T(8,128)}, u32[]{:S(2)}, u32[]{:S(2)}) collective-permute-start(f32[2,512,256]{2,1,0:T(8,128)S(1)} %slice_select_fusion.1), channel_id=1, source_target_pairs={{0,2},{1,3},{2,0},{3,1},{4,6},{5,7},{6,4},{7,5},{8,10},{9,11},{10,... | collective-permute-start | bytes 3145736 | tf_op jit(solution)/shard_map/ppermute | solution.py:12
  204.0 0.0 copy-done.9
  204.0 0.9 convolution_convert_fusion.1
  204.9 0.0 all-to-all-done
  204.9 0.2 reshape.86
  205.2 0.0 copy-start.2
  205.2 0.1 constant_dynamic-slice_fusion
  205.4 0.0 copy-start.4
  205.4 2.4 convolution_dynamic-update-slice_fusion
  207.8 0.0 copy-done.2
  207.8 0.4 fusion.29
  208.2 41.8 %collective-permute-done.4 = f32[2,512,256]{2,1,0:T(8,128)} collective-permute-done((f32[2,512,256]{2,1,0:T(8,128)S(1)}, f32[2,512,256]{2,1,0:T(8,128)}, u32[]{:S(2)}, u32[]{:S(2)}) %collective-permute-start.4) | collective-permute-done | bytes 1048608 | tf_op jit(solution)/shard_map/ppermute | solution.py:12
  250.1 0.0 copy-done.4
  250.1 1.4 select_add_fusion.1
  251.5 0.9 slice_select_fusion.2
  252.4 1.9 collective-permute-start.5
  254.3 0.6 fusion.4
  254.8 0.7 copy.33
  255.6 377.3 %all-reduce.1 = bf16[2,4,128,64]{2,3,1,0:T(8,128)(2,1)S(1)} all-reduce(f32[2,4,128,64]{2,3,1,0:T(8,128)S(1)} %convolution_dynamic-update-slice_fusion), channel_id=1, replica_groups=mesh['pipe'=8,'tensor'=64] {'tensor'}, use_global_device_ids=true, to_apply=%region_0.1 | all-reduce | flops 65536 | bytes 393216 | tf_op jit(solution)/shard_map/psum | solution.py:89
  632.9 1.2 fusion.11
  634.1 0.0 collective-permute-done.5
  634.1 1.2 fusion.6
  635.3 58.6 %collective-permute-start.6 = (bf16[2,512,128]{2,1,0:T(8,128)(2,1)S(1)}, bf16[2,512,128]{2,1,0:T(8,128)(2,1)S(1)}, u32[]{:S(2)}, u32[]{:S(2)}) collective-permute-start(bf16[2,512,128]{2,1,0:T(8,128)(2,1)S(1)} %fusion.6), channel_id=1, source_target_pairs={{64,0},{128,64},{192,128},{256,192},{320,256},{384,320},{448,384},... | collective-permute-start | bytes 786440 | tf_op jit(solution)/shard_map/ppermute | solution.py:18
  693.9 0.2 fusion.30
  694.1 0.6 fusion.5
  694.7 0.7 copy.32
  695.4 3.9 collective-permute-done.6
  699.3 0.7 copy.58
  (7 shorter events, 0.1 us)
Async XLA Ops:
  0.6 84.8 %copy-start = (bf16[1,1,1024,1024]{3,2,1,0:T(8,128)(2,1)S(1)}, bf16[1,1,1024,1024]{3,2,1,0:T(8,128)(2,1)}, u32[]{:S(2)}) copy-start(bf16[1,1,1024,1024]{3,2,1,0:T(8,128)(2,1)} %param.11) | copy-start | bytes 6291460
  2.6 9.1 %collective-permute-start = (bf16[2,64,1024]{2,1,0:T(8,128)(2,1)S(1)}, bf16[2,64,1024]{2,1,0:T(8,128)(2,1)S(1)}, u32[]{:S(2)}, u32[]{:S(2)}) collective-permute-start(bf16[2,64,1024]{2,1,0:T(8,128)(2,1)S(1)} %bitcast_select_fusion), channel_id=1, source_target_pairs={{0,8},{1,9},{2,10},{3,11},{4,12},{5,13},{6,14},{7,15},{8,0},{9,1},... | collective-permute-start | bytes 786440 | tf_op jit(solution)/shard_map/ppermute | solution.py:12
  11.8 4.7 copy-start.6
  11.8 15.5 %collective-permute-start.1 = (bf16[2,128,1024]{2,1,0:T(8,128)(2,1)S(1)}, bf16[2,128,1024]{2,1,0:T(8,128)(2,1)}, u32[]{:S(2)}, u32[]{:S(2)}) collective-permute-start(bf16[2,128,1024]{2,1,0:T(8,128)(2,1)S(1)} %maximum_select_fusion.2), channel_id=1, source_target_pairs={{0,16},{1,17},{2,18},{3,19},{4,20},{5,21},{6,22},{7,23},{8,24},{9,... | collective-permute-start | bytes 1572872 | tf_op jit(solution)/shard_map/ppermute | solution.py:12
  29.4 53.4 %collective-permute-start.2 = (bf16[2,256,1024]{2,1,0:T(8,128)(2,1)S(1)}, bf16[2,256,1024]{2,1,0:T(8,128)(2,1)}, u32[]{:S(2)}, u32[]{:S(2)}) collective-permute-start(bf16[2,256,1024]{2,1,0:T(8,128)(2,1)S(1)} %maximum_select_fusion.1), channel_id=1, source_target_pairs={{0,32},{1,33},{2,34},{3,35},{4,36},{5,37},{6,38},{7,39},{8,40},{9,... | collective-permute-start | bytes 3145736 | tf_op jit(solution)/shard_map/ppermute | solution.py:12
  85.4 2.4 copy-start.1
  87.8 2.8 copy-start.5
  87.8 13.4 %copy-start.11 = (bf16[1,2,8,64]{3,2,1,0:T(8,128)(2,1)S(1)}, bf16[1,2,8,64]{3,2,1,0:T(8,128)(2,1)}, u32[]{:S(2)}) copy-start(bf16[1,2,8,64]{3,2,1,0:T(8,128)(2,1)} %param.10) | copy-start | bytes 6148
  87.8 23.6 %copy-start.8 = (bf16[1,8,64,128]{3,2,1,0:T(8,128)(2,1)S(1)}, bf16[1,8,64,128]{3,2,1,0:T(8,128)(2,1)}, u32[]{:S(2)}) copy-start(bf16[1,8,64,128]{3,2,1,0:T(8,128)(2,1)} %param.12) | copy-start | bytes 393220
  87.8 23.6 %copy-start.10 = (s32[1,2,4]{2,1,0:T(2,128)S(1)}, s32[1,2,4]{2,1,0:T(2,128)}, u32[]{:S(2)}) copy-start(s32[1,2,4]{2,1,0:T(2,128)} %param.14) | copy-start | bytes 100
  90.6 61.9 %collective-permute-start.3 = (f32[2,512,512]{2,1,0:T(8,128)}, f32[2,512,512]{2,1,0:T(8,128)}, u32[]{:S(2)}, u32[]{:S(2)}) collective-permute-start(f32[2,512,512]{2,1,0:T(8,128)} %slice_select_fusion), channel_id=1, source_target_pairs={{0,4},{1,5},{2,6},{3,7},{4,0},{5,1},{6,2},{7,3},{8,12},{9,13},{10,... | collective-permute-start | bytes 6291464 | tf_op jit(solution)/shard_map/ppermute | solution.py:12
  102.1 102.9 %all-to-all-start = ((bf16[64,2,512]{2,1,0:T(2,128)(2,1)}), bf16[64,2,512]{2,1,0:T(2,128)(2,1)S(1)}, u32[]{:S(2)}, u32[]{:S(2)}) async-start(bf16[64,2,512]{2,1,0:T(2,128)(2,1)} %reshape.85), calls=%async_computation | async-start | bytes 262144 | tf_op jit(solution)/shard_map/all_to_all | solution.py:104
  156.0 1.3 copy-start.3
  157.4 46.7 %copy-start.9 = (bf16[1,1,8,8,1024]{4,3,2,1,0:T(8,128)(2,1)S(1)}, bf16[1,1,8,8,1024]{4,3,2,1,0:T(8,128)(2,1)}, u32[]{:S(2)}) copy-start(bf16[1,1,8,8,1024]{4,3,2,1,0:T(8,128)(2,1)} %param.13) | copy-start | bytes 393220
  157.5 92.5 %collective-permute-start.4 = (f32[2,512,256]{2,1,0:T(8,128)S(1)}, f32[2,512,256]{2,1,0:T(8,128)}, u32[]{:S(2)}, u32[]{:S(2)}) collective-permute-start(f32[2,512,256]{2,1,0:T(8,128)S(1)} %slice_select_fusion.1), channel_id=1, source_target_pairs={{0,2},{1,3},{2,0},{3,1},{4,6},{5,7},{6,4},{7,5},{8,10},{9,11},{10,... | collective-permute-start | bytes 3145736 | tf_op jit(solution)/shard_map/ppermute | solution.py:12
  205.2 2.6 copy-start.2
  205.4 44.7 %copy-start.4 = (f32[2,512,512]{2,1,0:T(8,128)S(1)}, f32[2,512,512]{2,1,0:T(8,128)}, u32[]{:S(2)}) copy-start(f32[2,512,512]{2,1,0:T(8,128)} %copy-done.3) | copy-start | bytes 6291460
  252.4 381.8 %collective-permute-start.5 = (f32[2,512,128]{2,1,0:T(8,128)}, f32[2,512,128]{2,1,0:T(8,128)}, u32[]{:S(2)}, u32[]{:S(2)}) collective-permute-start(f32[2,512,128]{2,1,0:T(8,128)} %slice_select_fusion.2), channel_id=1, source_target_pairs={{0,1},{1,0},{2,3},{3,2},{4,5},{5,4},{6,7},{7,6},{8,9},{9,8},{10,11... | collective-permute-start | bytes 1572872 | tf_op jit(solution)/shard_map/ppermute | solution.py:12
  632.9 61.0 %copy-start.7 = (bf16[1,2,512,128]{3,2,1,0:T(8,128)(2,1)S(1)}, bf16[1,2,512,128]{3,2,1,0:T(8,128)(2,1)}, u32[]{:S(2)}) copy-start(bf16[1,2,512,128]{3,2,1,0:T(8,128)(2,1)} %param.9) | copy-start | bytes 786436
  635.3 64.0 %collective-permute-start.6 = (bf16[2,512,128]{2,1,0:T(8,128)(2,1)S(1)}, bf16[2,512,128]{2,1,0:T(8,128)(2,1)S(1)}, u32[]{:S(2)}, u32[]{:S(2)}) collective-permute-start(bf16[2,512,128]{2,1,0:T(8,128)(2,1)S(1)} %fusion.6), channel_id=1, source_target_pairs={{64,0},{128,64},{192,128},{256,192},{320,256},{384,320},{448,384},... | collective-permute-start | bytes 786440 | tf_op jit(solution)/shard_map/ppermute | solution.py:18
